TPU v7x, 32 devices: a whole 2x2x4 slice. The times are simulated.
32 devices in a mesh: section: 2 (over core), blk: 8 (over z, y), head: 2 (over x).
Axes of the slice: x: 2, y: 2, z: 4, core: 2. Of those that a mesh axis runs over, the one named last changes fastest.
Arguments:
- projected: bfloat16 [8192, 8192], P(('section', 'blk')), may hold values from -6 to 6
- key_weight: bfloat16 [8192, 1024], P(None, 'head'), may hold values from -0.0625 to 0.0625
- value_weight: bfloat16 [8192, 1024], P(None, 'head'), may hold values from -0.0625 to 0.0625
- key_gain: float32 [128], replicated, may hold values from 0.1 to 1.9
- queries: bfloat16 [1024, 8, 1024], P('blk', 'section', 'head'), may hold values from -320 to 320
- frame_tokens: int32 [32], replicated, may hold values from 1 to 512, 8192 in all
- span_first: int32 [1024], replicated, may hold values from 0 to 31
- span_count: int32 [1024], replicated, may hold values from 1 to 32
Outputs:
- attended: bfloat16 [1024, 8, 1024], P('blk', 'section', 'head')
Inputs may be any that keep to these rules, and one draw needn't show every extreme that they name: Frame f holds frame_tokens[f] consecutive visual tokens, and they sum to 8192.
All inputs are finite; a program needn't handle non-finite values.
Results may differ from a plain program's by a relative error of at most 0.005.
The roundings to bfloat16 on the way count: a program that leaves them out, or rounds other values in their place, can miss the bound.
Values may be sent and summed in bfloat16 or wider, within the bound.
No kernel may reach another device: no remote copies, remote signals or barrier semaphores. Data moves between devices by JAX's collectives and lax.ppermute only.
A program may use at most 192 MiB of HBM per device.

v0:
```python
import jax
import jax.numpy as jnp
from jax import lax
from jax.sharding import PartitionSpec as P

HD = 128
FRAMES = 32


def span_bounds(frame_tokens, span_first, span_count):
    frame_ids = jnp.arange(FRAMES, dtype=jnp.int32)
    span_end = jnp.minimum(span_first + span_count, FRAMES)
    first_token = jnp.sum(
        jnp.where(frame_ids[None, :] < span_first[:, None], frame_tokens[None, :], 0), axis=1
    )
    end_token = jnp.sum(
        jnp.where(frame_ids[None, :] < span_end[:, None], frame_tokens[None, :], 0), axis=1
    )
    return (first_token, end_token)


def make_tables(projected, key_weight, value_weight, key_gain):
    count_rows = projected.shape[0]
    local_heads = key_weight.shape[1] // HD
    key_raw = jnp.dot(projected, key_weight, preferred_element_type=jnp.float32).reshape(
        count_rows, local_heads, HD
    )
    mean_square = jnp.mean(key_raw * key_raw, axis=2, keepdims=True)
    key_block = (key_raw / jnp.sqrt(mean_square + 1e-05) * key_gain).astype(jnp.bfloat16)
    value_block = (
        jnp.dot(projected, value_weight, preferred_element_type=jnp.float32)
        .astype(jnp.bfloat16)
        .reshape(count_rows, local_heads, HD)
    )
    return (key_block, value_block)


def masked_scores(query_block, key_block, key_positions, first_token, end_token):
    scores = jnp.einsum(
        "npgd,mgd->gnpm", query_block, key_block, preferred_element_type=jnp.float32
    ) * HD ** (-0.5)
    allowed = (key_positions[None, :] >= first_token[:, None]) & (
        key_positions[None, :] < end_token[:, None]
    )
    return jnp.where(allowed[None, :, None, :], scores, -1e30)


def weighted_sum(scores, row_max, value_block):
    weights = jnp.exp(scores - row_max[..., None])
    denominator = jnp.sum(weights, axis=3)
    numerator = jnp.einsum(
        "gnpm,mgd->npgd",
        weights.astype(jnp.bfloat16),
        value_block,
        preferred_element_type=jnp.float32,
    )
    return (numerator, jnp.transpose(denominator, (1, 2, 0)))


def body(
    projected, key_weight, value_weight, key_gain, queries, frame_tokens, span_first, span_count
):
    key_block, value_block = make_tables(projected, key_weight, value_weight, key_gain)
    first_token, end_token = span_bounds(frame_tokens, span_first, span_count)
    own_rows = queries.shape[0]
    sub_heads = queries.shape[1]
    local_heads = key_block.shape[1]
    count_rows = key_block.shape[0]
    section_count = lax.axis_size("section")
    block_count = lax.axis_size("blk")
    block_index = lax.axis_index("blk")
    section_ids = jnp.arange(section_count, dtype=jnp.int32)
    row_ids = jnp.arange(count_rows, dtype=jnp.int32)
    pair_keys, pair_values = (
        lax.all_gather(key_block, "section", axis=0, tiled=True),
        lax.all_gather(value_block, "section", axis=0, tiled=True),
    )
    all_keys, all_values = (
        lax.all_gather(pair_keys, "blk", axis=0, tiled=True),
        lax.all_gather(pair_values, "blk", axis=0, tiled=True),
    )
    block_ids = jnp.arange(block_count, dtype=jnp.int32)
    key_positions = (
        (section_ids[None, :, None] * block_count + block_ids[:, None, None]) * count_rows
        + row_ids[None, None, :]
    ).reshape(-1)
    own_first = lax.dynamic_slice_in_dim(first_token, block_index * own_rows, own_rows)
    own_end = lax.dynamic_slice_in_dim(end_token, block_index * own_rows, own_rows)
    shaped = queries.reshape(own_rows, sub_heads, local_heads, HD)
    scores = masked_scores(shaped, all_keys, key_positions, own_first, own_end)
    row_max = jnp.max(scores, axis=3)
    numerator, denominator = weighted_sum(scores, row_max, all_values)
    attended = numerator / denominator[..., None]
    return attended.astype(jnp.bfloat16).reshape(own_rows, sub_heads, local_heads * HD)


def solution(mesh):
    placed = (
        P(("section", "blk"), None),
        P(None, "head"),
        P(None, "head"),
        P(),
        P("blk", "section", "head"),
        P(),
        P(),
        P(),
    )
    return jax.shard_map(
        body, mesh=mesh, in_specs=placed, out_specs=P("blk", "section", "head"), check_vma=False
    )
```

profile of v0, /device:TPU:0, one launch (start us, length us, event | category | flops | bytes accessed | tf_op | source)
XLA Modules:
  0.0 328.6 jit_solution(8229665058144376835)
XLA Ops:
  6.5 9.5 %multiply_reduce_fusion = (f32[512,4]{0,1:T(4,128)S(1)}, f32[512,512]{0,1:T(8,128)S(1)}) fusion(bf16[512,8192]{1,0:T(8,128)(2,1)} %param.8, bf16[8192,512]{1,0:T(8,128)(2,1)} %param.9), kind=kOutput, calls=%fused_computation.16 | convolution fusion | flops 4295489536 | bytes 17833984 | tf_op jit(solution)/shard_map/dot_general | solution.py:25
  16.0 0.3 copy.17
  16.4 1.1 multiply_convert_fusion
  17.5 0.0 all-gather.9.cloned.1.call-update
  17.6 0.0 all-gather.5.cloned.1.call-start
  17.6 11.2 %convolution_convert_fusion = bf16[512,512]{0,1:T(8,128)(2,1)} fusion(bf16[512,8192]{1,0:T(8,128)(2,1)} %param.8, bf16[8192,512]{1,0:T(8,128)(2,1)} %param.10), kind=kOutput, calls=%fused_computation.12 | convolution fusion | flops 4295229440 | bytes 17301504 | tf_op jit(solution)/shard_map/dot_general | solution.py:31
  28.8 0.0 all-gather.5.cloned.1.call-update
  28.8 0.0 all-gather.11.cloned.1.call-start
  28.9 0.6 all-gather.9.cloned.1.call-done
  29.5 0.1 all-gather.11.cloned.1.call-update
  29.6 0.2 all-gather.7.cloned.1.call-start
  29.8 11.4 %all-gather.5.cloned.1.call-done = bf16[1024,4,128]{0,2,1:T(8,128)(2,1)} async-done(((bf16[512,4,128]{0,2,1:T(8,128)(2,1)}), bf16[1024,4,128]{0,2,1:T(8,128)(2,1)}) %all-gather.5.cloned.1.call-update) | async-done | bytes 1048592 | tf_op jit(solution)/shard_map/all_gather | solution.py:76
  41.3 0.1 select_reduce_fusion.1
  41.4 0.1 dynamic_slice.7
  41.5 0.1 dynamic_slice.6
  41.6 0.1 add_bitcast_fusion
  41.7 0.2 reshape.125
  41.9 3.7 %compare_and_fusion = pred[128,8192]{0,1:T(8,128)(4,1)S(1)} fusion(s32[128]{0:T(128)S(1)} %dynamic_slice.7, s32[128]{0:T(128)S(1)} %dynamic_slice.6, s32[8192]{0:T(1024)S(1)} %bitcast.54), kind=kLoop, calls=%fused_computation.10 | loop fusion | flops 3145728 | bytes 1082368 | tf_op jit(solution)/shard_map/and | solution.py:42
  45.6 123.4 %all-gather.11.cloned.1.call-done = bf16[8192,4,128]{2,0,1:T(8,128)(2,1)} async-done(((bf16[1024,4,128]{2,0,1:T(8,128)(2,1)}), bf16[8192,4,128]{2,0,1:T(8,128)(2,1)}) %all-gather.11.cloned.1.call-update) | async-done | bytes 8388624 | tf_op jit(solution)/shard_map/all_gather | solution.py:79
  169.1 28.2 %fusion.2 = (f32[4,128,4]{1,2,0:T(4,128)S(1)}, f32[4,8192,128,4]{2,1,3,0:T(8,128)}) fusion(pred[128,8192]{0,1:T(8,128)(4,1)S(1)} %compare_and_fusion, bf16[128,4,4,128]{3,2,1,0:T(4,128)(2,1)S(1)} %reshape.125, bf16[8192,4,128]{2,0,1:T(8,128)(2,1)} %all-gather.11.cloned.1.call-done), kind=kOutput, calls=%fused_computation.4 | convolution fusion | flops 4345296896 | bytes 77078528 | tf_op jit(solution)/shard_map/npgd,mgd->gnpm/dot_general | solution.py:39
  197.3 21.4 %fusion = f32[4,128,4]{1,2,0:T(4,128)S(1)} fusion(f32[4,8192,128,4]{2,1,3,0:T(8,128)} %get-tuple-element.10, f32[4,128,4]{1,2,0:T(4,128)S(1)} %get-tuple-element.9, pred[128,8192]{0,1:T(8,128)(4,1)S(1)} %compare_and_fusion), kind=kLoop, calls=%fused_computation.2 | loop fusion | flops 67106816 | bytes 68173824 | tf_op jit(solution)/shard_map/reduce_sum | solution.py:50
  218.7 75.1 %all-gather.7.cloned.1.call-done = bf16[8192,4,128]{0,2,1:T(8,128)(2,1)} async-done(((bf16[1024,4,128]{0,2,1:T(8,128)(2,1)}), bf16[8192,4,128]{0,2,1:T(8,128)(2,1)}) %all-gather.7.cloned.1.call-update) | async-done | bytes 8388624 | tf_op jit(solution)/shard_map/all_gather | solution.py:80
  293.8 27.0 %fusion.19 = bf16[128,4,4,128]{0,3,1,2:T(8,128)(2,1)S(1)} fusion(f32[4,8192,128,4]{2,1,3,0:T(8,128)} %get-tuple-element.10, f32[4,128,4]{1,2,0:T(4,128)S(1)} %get-tuple-element.9, pred[128,8192]{0,1:T(8,128)(4,1)S(1)} %compare_and_fusion, bf16[8192,4,128]{0,2,1:T(8,128)(2,1)} %all-gather.7.cloned.1.call-done, f32[128,4,4]{0,1,2:T(4,128)S(1)} %bitcast.55), kind=kOutput, calls=%fused_computation.14 | convolution fusion | flops 4362600448 | bytes 77086720 | tf_op jit(solution)/shard_map/gnpm,mgd->npgd/dot_general | solution.py:51
  320.8 1.2 copy.21
  (18 shorter events, 0.1 us)
Async XLA Ops:
  6.5 9.8 %copy-start.3 = (f32[128]{0:T(128)S(1)}, f32[128]{0:T(128)}, u32[]{:S(2)}) copy-start(f32[128]{0:T(128)} %param.11) | copy-start | bytes 1540
  6.5 22.9 %all-gather.9.cloned.1.call-start = ((), (), s32[]{:S(2)}) async-start(), calls=%async_computation.2 | async-start | bytes 1572864 | tf_op jit(solution)/shard_map/all_gather | solution.py:75
  17.5 23.7 %copy-start.1 = (s32[1024]{0:T(1024)S(1)}, s32[1024]{0:T(1024)}, u32[]{:S(2)}) copy-start(s32[1024]{0:T(1024)} %param.14) | copy-start | bytes 12292
  17.6 23.7 %copy-start.2 = (s32[1024]{0:T(1024)S(1)}, s32[1024]{0:T(1024)}, u32[]{:S(2)}) copy-start(s32[1024]{0:T(1024)} %param.15) | copy-start | bytes 12292
  17.6 23.7 %copy-start.4 = (s32[32]{0:T(128)S(1)}, s32[32]{0:T(128)}, u32[]{:S(2)}) copy-start(s32[32]{0:T(128)} %param.13) | copy-start | bytes 388
  17.6 24.1 %copy-start = (bf16[128,4,512]{2,1,0:T(4,128)(2,1)S(1)}, bf16[128,4,512]{2,1,0:T(4,128)(2,1)}, u32[]{:S(2)}) copy-start(bf16[128,4,512]{2,1,0:T(4,128)(2,1)} %param.12) | copy-start | bytes 1572868
  17.6 23.6 %all-gather.5.cloned.1.call-start = ((), (), s32[]{:S(2)}) async-start(), calls=%async_computation | async-start | bytes 1572864 | tf_op jit(solution)/shard_map/all_gather | solution.py:76
  28.8 140.3 %all-gather.11.cloned.1.call-start = ((), (), s32[]{:S(2)}) async-start(), calls=%async_computation.3 | async-start | bytes 9437184 | tf_op jit(solution)/shard_map/all_gather | solution.py:79
  29.6 264.2 %all-gather.7.cloned.1.call-start = ((), (), s32[]{:S(2)}) async-start(), calls=%async_computation.1 | async-start | bytes 9437184 | tf_op jit(solution)/shard_map/all_gather | solution.py:80
Sparse Core Ops, SparseCore 0:
  17.7 11.7 all-gather.8
  31.0 10.1 all-gather.4
  43.4 125.6 all-gather.10
  171.1 122.6 all-gather.6
where the time goes:
time: 329 us
  waiting for transfers between devices  211 us (64%)
  matrix products  75.8 us (23%)
  other arithmetic  26.5 us (8%)
  between operations  13.3 us (4%)
    all_gather x1, waiting for transfers between devices, body(): lax.all_gather(pair_keys, 'blk', axis=0, tiled=True)  123 us
    all_gather x1, waiting for transfers between devices, body(): lax.all_gather(pair_values, 'blk', axis=0, tiled=True)  75.1 us
    dot_general x1, matrix products, masked_scores(): jnp.einsum('npgd,mgd->gnpm', query_block, key_block, preferred_element_ty...  28.2 us
    dot_general x1, matrix products, weighted_sum(): jnp.einsum('gnpm,mgd->npgd', weights.astype(jnp.bfloat16), value_block, p...  27 us
    reduce_sum x1, other arithmetic, weighted_sum(): denominator = jnp.sum(weights, axis=3)  21.4 us
    all_gather x1, waiting for transfers between devices, body(): lax.all_gather(value_block, 'section', axis=0, tiled=True)  11.4 us
    dot_general x1, matrix products, make_tables(): jnp.dot(projected, value_weight, preferred_element_type=jnp.float32)  11.2 us
    dot_general x1, matrix products, make_tables(): jnp.dot(projected, key_weight, preferred_element_type=jnp.float32)  9.47 us
  transfers between devices with their start and end apart: 4, of which 4 were waited for; matrix products, arithmetic and copies ran while one was open for 20% of the time, Pallas kernels for 0%

commit v1 on v0

--- a/solution.py
+++ b/solution.py
@@ -75,9 +75,36 @@
         lax.all_gather(key_block, "section", axis=0, tiled=True),
         lax.all_gather(value_block, "section", axis=0, tiled=True),
     )
+
+    def write_the_sector(arr_in, dim_no=0):
+        e_now = lax.axis_size("blk")
+        w2 = lax.axis_index("blk")
+        reply, f_now, formed = (e_now, w2, arr_in.shape[dim_no])
+        in_order = [(j, (j + 1) % reply) for j in range(reply)]
+        trail = [(j, (j - 1) % reply) for j in range(reply)]
+        side_arr = jnp.zeros(
+            (*arr_in.shape[:dim_no], reply * formed, *arr_in.shape[dim_no + 1 :]), arr_in.dtype
+        )
+        side_arr = lax.dynamic_update_slice_in_dim(side_arr, arr_in, f_now * formed, axis=dim_no)
+        lower = y = arr_in
+        tall = reply // 2
+        pp = 1
+        while pp < tall + 1:
+            lower = lax.ppermute(lower, "blk", in_order)
+            side_arr = lax.dynamic_update_slice_in_dim(
+                side_arr, lower, (f_now - pp) % reply * formed, axis=dim_no
+            )
+            if pp < reply - tall:
+                y = lax.ppermute(y, "blk", trail)
+                side_arr = lax.dynamic_update_slice_in_dim(
+                    side_arr, y, (f_now + pp) % reply * formed, axis=dim_no
+                )
+            pp += 1
+        return side_arr
+
     all_keys, all_values = (
         lax.all_gather(pair_keys, "blk", axis=0, tiled=True),
-        lax.all_gather(pair_values, "blk", axis=0, tiled=True),
+        write_the_sector(pair_values),
     )
     block_ids = jnp.arange(block_count, dtype=jnp.int32)
     key_positions = (

time: 329 us -> 366 us (1.11)
  starting transfers between devices: 0.3 us -> 38.4 us
  waiting for transfers between devices: 211 us -> 190 us
  local copies, waits for them, and re-layouts: 1.94 us -> 22.9 us
    ppermute x0 -> x7, waiting for transfers between devices: none -> 177 us  [the longest x4 177 us: write_the_sector(): lower = lax.ppermute(lower, 'blk', in_order)]
    all_gather x1, waiting for transfers between devices: 123 us -> 0.01 us  [body(): lax.all_gather(pair_keys, 'blk', axis=0, tiled=True)]
    all_gather x1 -> x0, waiting for transfers between devices: 75.1 us -> none  [body(): lax.all_gather(pair_values, 'blk', axis=0, tiled=True)]
    ppermute x0 -> x7, starting transfers between devices: none -> 38.4 us  [the longest x3 29.2 us: write_the_sector(): y = lax.ppermute(y, 'blk', trail)]
    dynamic_update_slice x0 -> x8, local copies, waits for them, and re-layouts: none -> 14.7 us  [the longest x4 7.97 us: write_the_sector(): lax.dynamic_update_slice_in_dim(side_arr, lower, (f_now - pp) % reply * f...]
    broadcast_in_dim x0 -> x1, local copies, waits for them, and re-layouts: none -> 4.33 us  [write_the_sector(): jnp.zeros((*arr_in.shape[:dim_no], reply * formed, *arr_in.shape[dim_no +...]
  transfers between devices with their start and end apart: 4 -> 10, of which waited for: 4 -> 6; matrix products, arithmetic and copies ran while one was open for 20% -> 10% of each run, Pallas kernels for 0% -> 0%
where the time goes in v1:
time: 366 us
  waiting for transfers between devices  190 us (52%)
  matrix products  74.8 us (20%)
  starting transfers between devices  38.4 us (10%)
  other arithmetic  26.3 us (7%)
  local copies, waits for them, and re-layouts  22.9 us (6%)
  between operations  13.4 us (4%)
    ppermute x4, waiting for transfers between devices, write_the_sector(): lower = lax.ppermute(lower, 'blk', in_order)  177 us
    ppermute x3, starting transfers between devices, write_the_sector(): y = lax.ppermute(y, 'blk', trail)  29.2 us
    dot_general x1, matrix products, masked_scores(): jnp.einsum('npgd,mgd->gnpm', query_block, key_block, preferred_element_ty...  27.3 us
    dot_general x1, matrix products, weighted_sum(): jnp.einsum('gnpm,mgd->npgd', weights.astype(jnp.bfloat16), value_block, p...  26.9 us
    reduce_sum x1, other arithmetic, weighted_sum(): denominator = jnp.sum(weights, axis=3)  21.3 us
    all_gather x1, waiting for transfers between devices, body(): lax.all_gather(value_block, 'section', axis=0, tiled=True)  11.7 us
    dot_general x1, matrix products, make_tables(): jnp.dot(projected, value_weight, preferred_element_type=jnp.float32)  11.1 us
    dot_general x1, matrix products, make_tables(): jnp.dot(projected, key_weight, preferred_element_type=jnp.float32)  9.47 us
  transfers between devices with their start and end apart: 10, of which 6 were waited for; matrix products, arithmetic and copies ran while one was open for 10% of the time, Pallas kernels for 0%

profile of v1, /device:TPU:0, one launch (start us, length us, event | category | flops | bytes accessed | tf_op | source)
XLA Modules:
  0.0 365.7 jit_solution(6911607863355597410)
XLA Ops:
  6.5 9.5 %multiply_reduce_fusion = (f32[512,4]{0,1:T(4,128)S(1)}, f32[512,512]{0,1:T(8,128)S(1)}) fusion(bf16[512,8192]{1,0:T(8,128)(2,1)} %param.8, bf16[8192,512]{1,0:T(8,128)(2,1)} %param.9), kind=kOutput, calls=%fused_computation.16 | convolution fusion | flops 4295489536 | bytes 17833984 | tf_op jit(solution)/shard_map/dot_general | solution.py:25
  17.6 11.1 %convolution_convert_fusion = bf16[512,512]{0,1:T(8,128)(2,1)} fusion(bf16[512,8192]{1,0:T(8,128)(2,1)} %param.8, bf16[8192,512]{1,0:T(8,128)(2,1)} %param.10), kind=kOutput, calls=%fused_computation.12 | convolution fusion | flops 4295229440 | bytes 17301504 | tf_op jit(solution)/shard_map/dot_general | solution.py:31
  29.5 11.7 %all-gather.4.cloned.1.call-done = bf16[1024,4,128]{0,2,1:T(8,128)(2,1)} async-done(((bf16[512,4,128]{0,2,1:T(8,128)(2,1)}), bf16[1024,4,128]{0,2,1:T(8,128)(2,1)}) %all-gather.4.cloned.1.call-update) | async-done | bytes 1048592 | tf_op jit(solution)/shard_map/all_gather | solution.py:76
  43.0 3.0 collective-permute-start.1
  46.0 53.9 %collective-permute-done = bf16[1024,4,128]{0,2,1:T(8,128)(2,1)S(1)} collective-permute-done((bf16[1024,4,128]{0,2,1:T(8,128)(2,1)}, bf16[1024,4,128]{0,2,1:T(8,128)(2,1)S(1)}, u32[]{:S(2)}, u32[]{:S(2)}) %collective-permute-start) | collective-permute-done | bytes 1048608 | tf_op jit(solution)/shard_map/ppermute | solution.py:93
  99.9 2.4 collective-permute-start.2
  102.2 2.8 collective-permute-start.3
  105.1 61.6 %collective-permute-done.2 = bf16[1024,4,128]{0,2,1:T(8,128)(2,1)} collective-permute-done((bf16[1024,4,128]{0,2,1:T(8,128)(2,1)S(1)}, bf16[1024,4,128]{0,2,1:T(8,128)(2,1)}, u32[]{:S(2)}, u32[]{:S(2)}) %collective-permute-start.2) | collective-permute-done | bytes 1048608 | tf_op jit(solution)/shard_map/ppermute | solution.py:93
  166.7 2.6 collective-permute-start.4
  169.7 23.4 %collective-permute-start.5 = (bf16[1024,4,128]{0,2,1:T(8,128)(2,1)}, bf16[1024,4,128]{0,2,1:T(8,128)(2,1)}, u32[]{:S(2)}, u32[]{:S(2)}) collective-permute-start(bf16[1024,4,128]{0,2,1:T(8,128)(2,1)} %collective-permute-done.3), channel_id=1, source_target_pairs={{0,14},{2,0},{4,2},{6,4},{8,6},{10,8},{12,10},{14,12},{1,15},{3,1}... | collective-permute-start | bytes 3145736 | tf_op jit(solution)/shard_map/ppermute | solution.py:98
  193.1 41.0 %collective-permute-done.4 = bf16[1024,4,128]{0,2,1:T(8,128)(2,1)} collective-permute-done((bf16[1024,4,128]{0,2,1:T(8,128)(2,1)}, bf16[1024,4,128]{0,2,1:T(8,128)(2,1)}, u32[]{:S(2)}, u32[]{:S(2)}) %collective-permute-start.4) | collective-permute-done | bytes 1048608 | tf_op jit(solution)/shard_map/ppermute | solution.py:93
  234.1 2.5 collective-permute-start.6
  236.6 3.7 %compare_and_fusion = pred[128,8192]{0,1:T(8,128)(4,1)S(1)} fusion(s32[128]{0:T(128)S(1)} %dynamic_slice.7, s32[128]{0:T(128)S(1)} %dynamic_slice.6, s32[8192]{0:T(1024)S(1)} %bitcast.54), kind=kLoop, calls=%fused_computation.10 | loop fusion | flops 3145728 | bytes 1082368 | tf_op jit(solution)/shard_map/and | solution.py:42
  240.4 2.0 reshape.125
  242.5 4.3 %broadcast_in_dim.26 = bf16[8192,4,128]{0,2,1:T(8,128)(2,1)} broadcast(bf16[]{:T(256)} %constant.61.clone.1), dimensions={} | broadcast | bytes 8388610 | tf_op jit(solution)/shard_map/broadcast_in_dim | solution.py:85
  250.0 2.3 constant_dynamic-update-slice_fusion.4
  252.3 2.3 constant_dynamic-update-slice_fusion.3
  254.6 2.3 constant_dynamic-update-slice_fusion.2
  256.9 2.3 constant_dynamic-update-slice_fusion.1
  259.2 20.9 %collective-permute-done.6 = bf16[1024,4,128]{0,2,1:T(8,128)(2,1)} collective-permute-done((bf16[1024,4,128]{0,2,1:T(8,128)(2,1)}, bf16[1024,4,128]{0,2,1:T(8,128)(2,1)}, u32[]{:S(2)}, u32[]{:S(2)}) %collective-permute-start.6) | collective-permute-done | bytes 1048608 | tf_op jit(solution)/shard_map/ppermute | solution.py:93
  280.1 2.3 constant_dynamic-update-slice_fusion
  282.5 27.3 %fusion.2 = (f32[4,128,4]{1,2,0:T(4,128)S(1)}, f32[4,8192,128,4]{2,1,3,0:T(8,128)}) fusion(pred[128,8192]{0,1:T(8,128)(4,1)S(1)} %compare_and_fusion, bf16[128,4,4,128]{3,2,1,0:T(4,128)(2,1)S(1)} %copy-done.3, bf16[8192,4,128]{2,0,1:T(8,128)(2,1)} %all-gather.8.cloned.1.call-done), kind=kOutput, calls=%fused_computation.4 | convolution fusion | flops 4345296896 | bytes 77078528 | tf_op jit(solution)/shard_map/npgd,mgd->gnpm/dot_general | solution.py:39
  309.8 21.3 %fusion = f32[4,128,4]{1,2,0:T(4,128)S(1)} fusion(f32[4,8192,128,4]{2,1,3,0:T(8,128)} %get-tuple-element.10, f32[4,128,4]{1,2,0:T(4,128)S(1)} %get-tuple-element.9, pred[128,8192]{0,1:T(8,128)(4,1)S(1)} %compare_and_fusion), kind=kLoop, calls=%fused_computation.2 | loop fusion | flops 67106816 | bytes 68173824 | tf_op jit(solution)/shard_map/reduce_sum | solution.py:50
  331.0 26.9 %fusion.19 = bf16[128,4,4,128]{0,3,1,2:T(8,128)(2,1)S(1)} fusion(f32[4,8192,128,4]{2,1,3,0:T(8,128)} %get-tuple-element.10, f32[4,128,4]{1,2,0:T(4,128)S(1)} %get-tuple-element.9, pred[128,8192]{0,1:T(8,128)(4,1)S(1)} %compare_and_fusion, bf16[8192,4,128]{0,2,1:T(8,128)(2,1)} %constant_dynamic-update-slice_fusion, f32[128,4,4]{0,1,2:T(4,128)S(1)} %bitcast.55), kind=kOutput, calls=%fused_computation.14 | convolution fusion | flops 4362600448 | bytes 77086720 | tf_op jit(solution)/shard_map/gnpm,mgd->npgd/dot_general | solution.py:51
  (44 shorter events, 8.9 us)
Async XLA Ops:
  6.5 9.8 %copy-start.6 = (f32[128]{0:T(128)S(1)}, f32[128]{0:T(128)}, u32[]{:S(2)}) copy-start(f32[128]{0:T(128)} %param.11) | copy-start | bytes 1540
  6.5 22.9 %all-gather.6.cloned.1.call-start = ((), (), s32[]{:S(2)}) async-start(), calls=%async_computation.1 | async-start | bytes 1572864 | tf_op jit(solution)/shard_map/all_gather | solution.py:75
  17.5 151.7 %copy-start.4 = (s32[1024]{0:T(1024)S(1)}, s32[1024]{0:T(1024)}, u32[]{:S(2)}) copy-start(s32[1024]{0:T(1024)} %param.14) | copy-start | bytes 12292
  17.6 151.7 %copy-start.5 = (s32[1024]{0:T(1024)S(1)}, s32[1024]{0:T(1024)}, u32[]{:S(2)}) copy-start(s32[1024]{0:T(1024)} %param.15) | copy-start | bytes 12292
  17.6 151.7 %copy-start.7 = (s32[32]{0:T(128)S(1)}, s32[32]{0:T(128)}, u32[]{:S(2)}) copy-start(s32[32]{0:T(128)} %param.13) | copy-start | bytes 388
  17.6 23.6 %all-gather.4.cloned.1.call-start = ((), (), s32[]{:S(2)}) async-start(), calls=%async_computation | async-start | bytes 1572864 | tf_op jit(solution)/shard_map/all_gather | solution.py:76
  28.8 253.7 %all-gather.8.cloned.1.call-start = ((), (), s32[]{:S(2)}) async-start(), calls=%async_computation.2 | async-start | bytes 9437184 | tf_op jit(solution)/shard_map/all_gather | solution.py:106
  41.2 205.6 %copy-start = (bf16[1024,4,128]{0,2,1:T(8,128)(2,1)S(1)}, bf16[1024,4,128]{0,2,1:T(8,128)(2,1)}, u32[]{:S(2)}) copy-start(bf16[1024,4,128]{0,2,1:T(8,128)(2,1)} %all-gather.4.cloned.1.call-done) | copy-start | bytes 3145732
  41.2 58.6 %collective-permute-start = (bf16[1024,4,128]{0,2,1:T(8,128)(2,1)}, bf16[1024,4,128]{0,2,1:T(8,128)(2,1)S(1)}, u32[]{:S(2)}, u32[]{:S(2)}) collective-permute-start(bf16[1024,4,128]{0,2,1:T(8,128)(2,1)} %all-gather.4.cloned.1.call-done), channel_id=1, source_target_pairs={{0,2},{2,4},{4,6},{6,8},{8,10},{10,12},{12,14},{14,0},{1,3},{3,5},... | collective-permute-start | bytes 3145736 | tf_op jit(solution)/shard_map/ppermute | solution.py:93
  43.0 59.3 %collective-permute-start.1 = (bf16[1024,4,128]{0,2,1:T(8,128)(2,1)}, bf16[1024,4,128]{0,2,1:T(8,128)(2,1)S(1)}, u32[]{:S(2)}, u32[]{:S(2)}) collective-permute-start(bf16[1024,4,128]{0,2,1:T(8,128)(2,1)} %all-gather.4.cloned.1.call-done), channel_id=1, source_target_pairs={{0,14},{2,0},{4,2},{6,4},{8,6},{10,8},{12,10},{14,12},{1,15},{3,1}... | collective-permute-start | bytes 3145736 | tf_op jit(solution)/shard_map/ppermute | solution.py:98
  99.9 66.8 %collective-permute-start.2 = (bf16[1024,4,128]{0,2,1:T(8,128)(2,1)S(1)}, bf16[1024,4,128]{0,2,1:T(8,128)(2,1)}, u32[]{:S(2)}, u32[]{:S(2)}) collective-permute-start(bf16[1024,4,128]{0,2,1:T(8,128)(2,1)S(1)} %collective-permute-done), channel_id=1, source_target_pairs={{0,2},{2,4},{4,6},{6,8},{8,10},{10,12},{12,14},{14,0},{1,3},{3,5},... | collective-permute-start | bytes 3145736 | tf_op jit(solution)/shard_map/ppermute | solution.py:93
  102.2 134.3 %copy-start.1 = (bf16[1024,4,128]{0,2,1:T(8,128)(2,1)}, bf16[1024,4,128]{0,2,1:T(8,128)(2,1)S(1)}, u32[]{:S(2)}) copy-start(bf16[1024,4,128]{0,2,1:T(8,128)(2,1)S(1)} %collective-permute-done.1) | copy-start | bytes 3145732
  102.2 67.4 %collective-permute-start.3 = (bf16[1024,4,128]{0,2,1:T(8,128)(2,1)S(1)}, bf16[1024,4,128]{0,2,1:T(8,128)(2,1)}, u32[]{:S(2)}, u32[]{:S(2)}) collective-permute-start(bf16[1024,4,128]{0,2,1:T(8,128)(2,1)S(1)} %collective-permute-done.1), channel_id=1, source_target_pairs={{0,14},{2,0},{4,2},{6,4},{8,6},{10,8},{12,10},{14,12},{1,15},{3,1}... | collective-permute-start | bytes 3145736 | tf_op jit(solution)/shard_map/ppermute | solution.py:98
  166.7 67.4 %collective-permute-start.4 = (bf16[1024,4,128]{0,2,1:T(8,128)(2,1)}, bf16[1024,4,128]{0,2,1:T(8,128)(2,1)}, u32[]{:S(2)}, u32[]{:S(2)}) collective-permute-start(bf16[1024,4,128]{0,2,1:T(8,128)(2,1)} %collective-permute-done.2), channel_id=1, source_target_pairs={{0,2},{2,4},{4,6},{6,8},{8,10},{10,12},{12,14},{14,0},{1,3},{3,5},... | collective-permute-start | bytes 3145736 | tf_op jit(solution)/shard_map/ppermute | solution.py:93
  169.7 87.2 %collective-permute-start.5 = (bf16[1024,4,128]{0,2,1:T(8,128)(2,1)}, bf16[1024,4,128]{0,2,1:T(8,128)(2,1)}, u32[]{:S(2)}, u32[]{:S(2)}) collective-permute-start(bf16[1024,4,128]{0,2,1:T(8,128)(2,1)} %collective-permute-done.3), channel_id=1, source_target_pairs={{0,14},{2,0},{4,2},{6,4},{8,6},{10,8},{12,10},{14,12},{1,15},{3,1}... | collective-permute-start | bytes 3145736 | tf_op jit(solution)/shard_map/ppermute | solution.py:98
  234.1 46.0 %collective-permute-start.6 = (bf16[1024,4,128]{0,2,1:T(8,128)(2,1)}, bf16[1024,4,128]{0,2,1:T(8,128)(2,1)}, u32[]{:S(2)}, u32[]{:S(2)}) collective-permute-start(bf16[1024,4,128]{0,2,1:T(8,128)(2,1)} %collective-permute-done.4), channel_id=1, source_target_pairs={{0,2},{2,4},{4,6},{6,8},{8,10},{10,12},{12,14},{14,0},{1,3},{3,5},... | collective-permute-start | bytes 3145736 | tf_op jit(solution)/shard_map/ppermute | solution.py:93
  242.5 6.5 %copy-start.2 = (bf16[1024,4,128]{0,2,1:T(8,128)(2,1)S(1)}, bf16[1024,4,128]{0,2,1:T(8,128)(2,1)}, u32[]{:S(2)}) copy-start(bf16[1024,4,128]{0,2,1:T(8,128)(2,1)} %copy-done.1) | copy-start | bytes 3145732
  247.9 34.6 %copy-start.3 = (bf16[128,4,4,128]{3,2,1,0:T(4,128)(2,1)S(1)}, bf16[128,4,4,128]{3,2,1,0:T(4,128)(2,1)}, u32[]{:S(2)}) copy-start(bf16[128,4,4,128]{3,2,1,0:T(4,128)(2,1)} %reshape.125) | copy-start | bytes 1572868
Sparse Core Ops, SparseCore 0:
  17.7 11.7 all-gather.5
  31.0 10.1 all-gather.3
  43.4 227.8 all-gather.7
